TPU v7x, 256 devices: a whole 4x4x8 slice. The times are simulated.
256 devices in a mesh: ep: 64 (over z, x, core), tp: 4 (over y).
Axes of the slice: x: 4, y: 4, z: 8, core: 2. Of those that a mesh axis runs over, the one named last changes fastest.
Arguments:
- tokens: bfloat16 [16384, 3584], P('ep', 'tp'), may hold values from -6 to 6
- grad_out: bfloat16 [16384, 3584], P('ep', 'tp'), may hold values from -6 to 6
- route_ids: int32 [16384, 2], P('ep'), may hold values from 0 to 63, all different within a row; in each aligned block of 256 rows (0 to 255, 256 to 511, ...) at most 16 rows name the same one
- route_probs: float32 [16384, 2], P('ep'), may hold values from 0.2 to 1
- w_gate: bfloat16 [64, 3584, 1024], P('ep', None, 'tp'), may hold values from -0.09375 to 0.09375
- w_up: bfloat16 [64, 3584, 1024], P('ep', None, 'tp'), may hold values from -0.09375 to 0.09375
- w_down: bfloat16 [64, 1024, 3584], P('ep', 'tp'), may hold values from -0.1875 to 0.1875
Outputs:
- grad_tokens: bfloat16 [16384, 3584], P('ep', 'tp')
- grad_gate: bfloat16 [64, 3584, 1024], P('ep', None, 'tp')
- grad_up: bfloat16 [64, 3584, 1024], P('ep', None, 'tp')
- grad_down: bfloat16 [64, 1024, 3584], P('ep', 'tp')
Inputs may be any that keep to these rules, and one draw needn't show every extreme that they name: `route_ids`: each token names 2 different experts. Among the tokens of one index of ep (aligned blocks of 256 tokens), no expert is named by more than 16 tokens, and in every draw some expert is named by exactly 16 of some block.
All inputs are finite; a program needn't handle non-finite values.
Results may differ from a plain program's by a relative error of at most 0.0065.
Values may be sent and summed in bfloat16 or wider, within the bound.
No kernel may reach another device: no remote copies, remote signals or barrier semaphores. Data moves between devices by JAX's collectives and lax.ppermute only.
A program may use at most 128 MiB of HBM per device.

v0:
```python
import jax
import jax.numpy as jnp
from jax import lax
from jax.sharding import PartitionSpec as P


def contract_last(left, right):
    return lax.dot_general(
        left, right, (((1,), (1,)), ((), ())), preferred_element_type=jnp.float32
    )


def contract_first(left, right):
    return lax.dot_general(
        left, right, (((0,), (0,)), ((), ())), preferred_element_type=jnp.float32
    )


def row_pass(x_rows, s_rows, gate_cols, up_cols, down_rows):
    gate = jnp.dot(x_rows, gate_cols, preferred_element_type=jnp.float32)
    upper = jnp.dot(x_rows, up_cols, preferred_element_type=jnp.float32)
    sigma = jax.nn.sigmoid(gate)
    active = gate * sigma
    hidden = (active * upper).astype(jnp.bfloat16)
    back = contract_last(s_rows, down_rows)
    d_up = (back * active).astype(jnp.bfloat16)
    d_gate = (back * upper * sigma * (1.0 + gate * (1.0 - sigma))).astype(jnp.bfloat16)
    return (
        d_gate,
        d_up,
        contract_first(x_rows, d_gate),
        contract_first(x_rows, d_up),
        contract_first(hidden, s_rows),
    )


def per_device(tokens, grad_out, route_ids, route_probs, w_gate, w_up, w_down):
    n_src = lax.axis_size("ep")
    tok_rows, quarter = tokens.shape
    top = route_ids.shape[1]
    width = w_gate.shape[1]
    cap = max(2, 2 * tok_rows * top // n_src)
    total_rows = n_src * cap
    gate_cols = w_gate[0]
    up_cols = w_up[0]
    down_rows = w_down[0]
    flat_ids = route_ids.reshape(-1)
    routes = flat_ids.shape[0]
    onehot = (flat_ids[:, None] == jnp.arange(n_src, dtype=jnp.int32)[None, :]).astype(jnp.int32)
    rank = jnp.sum((jnp.cumsum(onehot, axis=0) - onehot) * onehot, axis=1)
    slot = flat_ids * cap + rank
    route_of = (
        jnp.full((n_src * cap,), routes, jnp.int32)
        .at[slot]
        .set(jnp.arange(routes, dtype=jnp.int32))
    )
    filled = route_of < routes
    token_of = jnp.where(filled, route_of // top, tok_rows)
    x_send = jnp.take(tokens, token_of, axis=0, mode="fill", fill_value=0).reshape(
        n_src, cap, quarter
    )
    scaled = (route_probs[:, :, None] * grad_out[:, None, :].astype(jnp.float32)).astype(
        jnp.bfloat16
    )
    s_send = jnp.take(
        scaled.reshape(routes, quarter), route_of, axis=0, mode="fill", fill_value=0
    ).reshape(n_src, cap, quarter)
    x_recv, s_recv = (
        lax.all_to_all(x_send, "ep", split_axis=0, concat_axis=0, tiled=True),
        lax.all_to_all(s_send, "ep", split_axis=0, concat_axis=0, tiled=True),
    )
    x_full, s_full = (
        lax.all_gather(x_recv, "tp", axis=2, tiled=True),
        lax.all_gather(s_recv, "tp", axis=2, tiled=True),
    )
    x_rows = x_full.reshape(total_rows, width)
    s_rows = s_full.reshape(total_rows, width)
    d_gate, d_up, g_gate, g_up, g_down = row_pass(x_rows, s_rows, gate_cols, up_cols, down_rows)
    part = contract_last(d_gate, gate_cols) + contract_last(d_up, up_cols)
    dx_rows = lax.psum_scatter(part, "tp", scatter_dimension=1, tiled=True)
    dx_rows = dx_rows.astype(jnp.bfloat16)
    back_slots = lax.all_to_all(
        dx_rows.reshape(n_src, cap, quarter), "ep", split_axis=0, concat_axis=0, tiled=True
    )
    per_route = jnp.take(back_slots.reshape(n_src * cap, quarter), slot, axis=0)
    grad_tokens = jnp.sum(
        per_route.reshape(tok_rows, top, quarter).astype(jnp.float32), axis=1
    ).astype(jnp.bfloat16)
    return (
        grad_tokens,
        g_gate.astype(jnp.bfloat16)[None],
        g_up.astype(jnp.bfloat16)[None],
        g_down.astype(jnp.bfloat16)[None],
    )


def solution(mesh):
    placed = (
        P("ep", "tp"),
        P("ep", "tp"),
        P("ep", None),
        P("ep", None),
        P("ep", None, "tp"),
        P("ep", None, "tp"),
        P("ep", "tp", None),
    )
    return jax.shard_map(
        per_device,
        mesh=mesh,
        in_specs=placed,
        out_specs=(P("ep", "tp"), P("ep", None, "tp"), P("ep", None, "tp"), P("ep", "tp", None)),
        check_vma=False,
    )
```

profile of v0, /device:TPU:2, one launch (start us, length us, event | category | flops | bytes accessed | tf_op | source)
XLA Modules:
  0.0 459.1 jit_solution(468386669442834185)
XLA Ops:
  11.1 2.4 scatter_custom_fusion
  13.7 5.3 %gather_fusion.1 = bf16[1024,896]{1,0:T(8,128)(2,1)} fusion(bf16[256,896]{1,0:T(8,128)(2,1)S(1)} %copy-done.2, s32[1024]{0:T(1024)S(1)} %get-tuple-element.9), kind=kCustom, calls=%fused_computation.1 | custom fusion | bytes 3674112 | tf_op jit(solution)/shard_map/jit(_take)/gather | solution.py:59
  19.0 1.8 broadcast_select_fusion
  20.8 57.5 %all_to_all.15 = bf16[64,16,896]{2,1,0:T(8,128)(2,1)} all-to-all(bf16[64,16,896]{2,1,0:T(8,128)(2,1)S(1)} %broadcast_select_fusion), channel_id=1, replica_groups=mesh['ep'=64,'tp'=4] {'ep'}, dimensions={0} | all-to-all | bytes 3670016 | tf_op jit(solution)/shard_map/all_to_all | solution.py:69
  81.1 3.4 mul.68
  86.1 5.3 %gather_fusion = bf16[1024,896]{1,0:T(8,128)(2,1)} fusion(bf16[512,896]{1,0:T(8,128)(2,1)S(1)} %multiply_convert_fusion, s32[1024]{0:T(1024)S(1)} %get-tuple-element.8), kind=kCustom, calls=%fused_computation | custom fusion | bytes 3674112 | tf_op jit(solution)/shard_map/jit(_take)/gather | solution.py:65
  91.4 1.9 broadcast_select_fusion.1
  93.3 51.0 %all_to_all.16 = bf16[64,16,896]{2,1,0:T(8,128)(2,1)} all-to-all(bf16[64,16,896]{2,1,0:T(8,128)(2,1)S(1)} %broadcast_select_fusion.1), channel_id=1, replica_groups=mesh['ep'=64,'tp'=4] {'ep'}, dimensions={0} | all-to-all | bytes 3670016 | tf_op jit(solution)/shard_map/all_to_all | solution.py:70
  144.6 7.2 %all-gather.5.cloned.1.call-done = bf16[64,16,3584]{2,1,0:T(8,128)(2,1)} async-done(((bf16[64,16,896]{2,1,0:T(8,128)(2,1)}), bf16[64,16,3584]{2,1,0:T(8,128)(2,1)}) %all-gather.5.cloned.1.call-update) | async-done | bytes 7340048 | tf_op jit(solution)/shard_map/all_gather | solution.py:73
  151.8 6.3 %fusion.5 = f32[1024,256]{1,0:T(8,128)} fusion(bf16[1024,3584]{1,0:T(8,128)(2,1)} %bitcast.64, bf16[1,3584,256]{2,1,0:T(8,128)(2,1)S(1)} %copy-done), kind=kOutput, calls=%fused_computation.13 | convolution fusion | flops 1879048192 | bytes 10223616 | tf_op jit(solution)/shard_map/dot_general | solution.py:20
  158.1 3.1 fusion.8
  161.1 70.3 %all-gather.3.cloned.1.call-done = bf16[64,16,3584]{2,1,0:T(8,128)(2,1)} async-done(((bf16[64,16,896]{2,1,0:T(8,128)(2,1)}), bf16[64,16,3584]{2,1,0:T(8,128)(2,1)}) %all-gather.3.cloned.1.call-update) | async-done | bytes 7340048 | tf_op jit(solution)/shard_map/all_gather | solution.py:74
  231.4 6.4 %multiply_convert_fusion.2 = (bf16[1024,256]{1,0:T(8,128)(2,1)S(1)}, bf16[1024,256]{1,0:T(8,128)(2,1)S(1)}) fusion(f32[1024,256]{1,0:T(8,128)} %fusion.5, f32[1024,256]{1,0:T(8,128)} %fusion.8, bf16[1024,3584]{1,0:T(8,128)(2,1)} %bitcast.68, bf16[1,256,3584]{2,1,0:T(8,128)(2,1)} %param.13), kind=kOutput, calls=%fused_computation.25 | convolution fusion | flops 1882456064 | bytes 12320768 | tf_op jit(solution)/shard_map/dot_general | solution.py:8
  237.8 2.1 fusion.3
  240.0 7.6 %convolution_add_fusion = f32[1024,3584]{1,0:T(8,128)} fusion(f32[1024,3584]{1,0:T(8,128)S(1)} %fusion.3, bf16[1024,256]{1,0:T(8,128)(2,1)S(1)} %get-tuple-element.4, bf16[1,3584,256]{2,1,0:T(8,128)(2,1)S(1)} %copy-done.4), kind=kOutput, calls=%fused_computation.4 | convolution fusion | flops 1882718208 | bytes 31719424 | tf_op jit(solution)/shard_map/dot_general | solution.py:8
  247.6 135.1 %reduce-scatter.2.cloned.1.call-done = f32[1024,896]{1,0:T(8,128)} async-done(((f32[1024,3584]{1,0:T(8,128)}), f32[1024,896]{1,0:T(8,128)}) %reduce-scatter.2.cloned.1.call-update) | async-done | bytes 3670032 | tf_op jit(solution)/shard_map/reduce_scatter | solution.py:80
  382.7 3.5 convert_element_type.44
  386.2 10.9 %all-to-all-start.2 = ((bf16[64,16,896]{2,1,0:T(8,128)(2,1)}), bf16[64,16,896]{2,1,0:T(8,128)(2,1)}, u32[]{:S(2)}, u32[]{:S(2)}) async-start(bf16[64,16,896]{2,1,0:T(8,128)(2,1)} %bitcast.10), calls=%async_computation.3 | async-start | bytes 3670016 | tf_op jit(solution)/shard_map/all_to_all | solution.py:82
  397.5 6.6 %fusion.1 = bf16[1,3584,256]{2,1,0:T(8,128)(2,1)} fusion(bf16[1024,3584]{1,0:T(8,128)(2,1)} %bitcast.65, bf16[1024,256]{1,0:T(8,128)(2,1)S(1)} %get-tuple-element.4), kind=kOutput, calls=%fused_computation.9 | convolution fusion | flops 1879965696 | bytes 9699328 | tf_op jit(solution)/shard_map/dot_general | solution.py:14
  404.1 6.6 %fusion = bf16[1,3584,256]{2,1,0:T(8,128)(2,1)} fusion(bf16[1024,3584]{1,0:T(8,128)(2,1)} %bitcast.66, bf16[1024,256]{1,0:T(8,128)(2,1)S(1)} %get-tuple-element.5), kind=kOutput, calls=%fused_computation.8 | convolution fusion | flops 1879965696 | bytes 9699328 | tf_op jit(solution)/shard_map/dot_general | solution.py:14
  410.7 3.4 fusion.2
  414.1 28.5 %all-to-all-done.2 = bf16[64,16,896]{2,1,0:T(8,128)(2,1)} async-done(((bf16[64,16,896]{2,1,0:T(8,128)(2,1)}), bf16[64,16,896]{2,1,0:T(8,128)(2,1)}, u32[]{:S(2)}, u32[]{:S(2)}) %all-to-all-start.2) | async-done | bytes 1835040 | tf_op jit(solution)/shard_map/all_to_all | solution.py:82
  442.6 4.4 gather_fusion.2
  448.3 4.3 fusion.13
  (61 shorter events, 10.4 us)
Async XLA Ops:
  7.2 144.6 %copy-start = (bf16[1,3584,256]{2,1,0:T(8,128)(2,1)S(1)}, bf16[1,3584,256]{2,1,0:T(8,128)(2,1)}, u32[]{:S(2)}) copy-start(bf16[1,3584,256]{2,1,0:T(8,128)(2,1)} %param.11) | copy-start | bytes 5505028
  7.2 6.5 %copy-start.2 = (bf16[256,896]{1,0:T(8,128)(2,1)S(1)}, bf16[256,896]{1,0:T(8,128)(2,1)}, u32[]{:S(2)}) copy-start(bf16[256,896]{1,0:T(8,128)(2,1)} %param.7) | copy-start | bytes 1376260
  7.2 144.6 %all-gather.5.cloned.1.call-start = ((), (), s32[]{:S(2)}) async-start(), calls=%async_computation.5 | async-start | bytes 9175040 | tf_op jit(solution)/shard_map/all_gather | solution.py:73
  78.3 0.7 copy-start.7
  78.3 1.0 copy-start.5
  78.4 153.0 %all-gather.3.cloned.1.call-start = ((), (), s32[]{:S(2)}) async-start(), calls=%async_computation.4 | async-start | bytes 9175040 | tf_op jit(solution)/shard_map/all_gather | solution.py:74
  144.4 238.3 %reduce-scatter.2.cloned.1.call-start = ((), (), s32[]{:S(2)}) async-start(), calls=%async_computation.6 | async-start | bytes 18350080 | tf_op jit(solution)/shard_map/reduce_scatter | solution.py:80
  151.8 6.3 %copy-start.3 = (bf16[1,3584,256]{2,1,0:T(8,128)(2,1)S(1)}, bf16[1,3584,256]{2,1,0:T(8,128)(2,1)}, u32[]{:S(2)}) copy-start(bf16[1,3584,256]{2,1,0:T(8,128)(2,1)} %param.12) | copy-start | bytes 5505028
  151.8 6.3 %copy-start.8 = (bf16[64,16,3584]{2,1,0:T(8,128)(2,1)S(1)}, bf16[64,16,3584]{2,1,0:T(8,128)(2,1)}, u32[]{:S(2)}) copy-start(bf16[64,16,3584]{2,1,0:T(8,128)(2,1)} %all-gather.5.cloned.1.call-done) | copy-start | bytes 22020100
  237.8 2.1 copy-start.4
  386.2 11.1 %copy-start.6 = (s32[256,2]{0,1:T(2,128)S(1)}, s32[256,2]{0,1:T(2,128)}, u32[]{:S(2)}) copy-start(s32[256,2]{0,1:T(2,128)} %param.9) | copy-start | bytes 6148
  386.2 56.4 %all-to-all-start.2 = ((bf16[64,16,896]{2,1,0:T(8,128)(2,1)}), bf16[64,16,896]{2,1,0:T(8,128)(2,1)}, u32[]{:S(2)}, u32[]{:S(2)}) async-start(bf16[64,16,896]{2,1,0:T(8,128)(2,1)} %bitcast.10), calls=%async_computation.3 | async-start | bytes 3670016 | tf_op jit(solution)/shard_map/all_to_all | solution.py:82
  397.5 13.2 %slice-start = ((s8[7340032]{0:T(1024)(128)(4,1)}), s8[4194304]{0:T(1024)(128)(4,1)S(1)}, s32[]{:S(2)}) async-start(s8[7340032]{0:T(1024)(128)(4,1)} %bitcast.69), calls=%async_computation.7 | async-start | bytes 8388608
  404.1 6.6 %slice-start.1 = ((s8[7340032]{0:T(1024)(128)(4,1)}), s8[3145728]{0:T(1024)(128)(4,1)S(1)}, s32[]{:S(2)}) async-start(s8[7340032]{0:T(1024)(128)(4,1)} %bitcast.69), calls=%async_computation.8 | async-start | bytes 6291456
  404.1 6.6 %copy-start.9 = (f32[1024,256]{1,0:T(8,128)S(1)}, f32[1024,256]{1,0:T(8,128)}, u32[]{:S(2)}) copy-start(f32[1024,256]{1,0:T(8,128)} %fusion.5) | copy-start | bytes 3145732
  404.1 6.6 %copy-start.10 = (f32[1024,256]{1,0:T(8,128)S(1)}, f32[1024,256]{1,0:T(8,128)}, u32[]{:S(2)}) copy-start(f32[1024,256]{1,0:T(8,128)} %fusion.8) | copy-start | bytes 3145732
  442.6 10.0 %copy-start.1 = (bf16[1,3584,256]{2,1,0:T(8,128)(2,1)S(1)}, bf16[1,3584,256]{2,1,0:T(8,128)(2,1)}, u32[]{:S(2)}) copy-start(bf16[1,3584,256]{2,1,0:T(8,128)(2,1)} %param.11) | copy-start | bytes 5505028
Sparse Core Ops, SparseCore 0:
  78.5 73.2 all-gather.4
  153.6 77.7 all-gather.2
  247.7 134.8 reduce-scatter.1
where the time goes:
time: 460 us; the launch traced here: 459 us
  waiting for transfers between devices  241 us (52%)
  blocking collectives  109 us (24%)
  matrix products  42 us (9%)
  local copies, waits for them, and re-layouts  26.8 us (6%)
  other arithmetic  15.5 us (3%)
  between operations  14 us (3%)
  starting transfers between devices  11.2 us (2%)
    reduce_scatter x1, waiting for transfers between devices, per_device(): dx_rows = lax.psum_scatter(part, 'tp', scatter_dimension=1, tiled=True)  135 us
    all_gather x1, waiting for transfers between devices, per_device(): lax.all_gather(s_recv, 'tp', axis=2, tiled=True)  70.3 us
    all_to_all x1, blocking collectives, per_device(): lax.all_to_all(x_send, 'ep', split_axis=0, concat_axis=0, tiled=True)  57.5 us
    all_to_all x1, blocking collectives, per_device(): lax.all_to_all(s_send, 'ep', split_axis=0, concat_axis=0, tiled=True)  51 us
    all_to_all x1, waiting for transfers between devices, per_device(): lax.all_to_all(dx_rows.reshape(n_src, cap, quarter), 'ep', split_axis=0,...  28.5 us
    dot_general x3, matrix products, contract_first(): lax.dot_general(left, right, (((0,), (0,)), ((), ())), preferred_element_...  16.6 us
    dot_general x3, matrix products, contract_last(): lax.dot_general(left, right, (((1,), (1,)), ((), ())), preferred_element_...  16.2 us
    all_to_all x1, starting transfers between devices, per_device(): lax.all_to_all(dx_rows.reshape(n_src, cap, quarter), 'ep', split_axis=0,...  10.9 us
  transfers between devices with their start and end apart: 4, of which 4 were waited for; matrix products, arithmetic and copies ran while one was open for 9% of the time, Pallas kernels for 0%

commit v1 on v0

--- a/solution.py
+++ b/solution.py
@@ -35,6 +35,14 @@
 
 
 def per_device(tokens, grad_out, route_ids, route_probs, w_gate, w_up, w_down):
+
+    def hold_the_tokens(tile_in, pos_dim=2):
+        local_next = lax.axis_size("tp")
+        finding = jnp.stack([tile_in] * local_next, axis=0)
+        front = lax.all_to_all(finding, axis_name="tp", split_axis=0, concat_axis=0)
+        parts_out = jnp.concatenate(front, axis=pos_dim)
+        return parts_out
+
     n_src = lax.axis_size("ep")
     tok_rows, quarter = tokens.shape
     top = route_ids.shape[1]
@@ -69,10 +77,7 @@
         lax.all_to_all(x_send, "ep", split_axis=0, concat_axis=0, tiled=True),
         lax.all_to_all(s_send, "ep", split_axis=0, concat_axis=0, tiled=True),
     )
-    x_full, s_full = (
-        lax.all_gather(x_recv, "tp", axis=2, tiled=True),
-        lax.all_gather(s_recv, "tp", axis=2, tiled=True),
-    )
+    x_full, s_full = (lax.all_gather(x_recv, "tp", axis=2, tiled=True), hold_the_tokens(s_recv))
     x_rows = x_full.reshape(total_rows, width)
     s_rows = s_full.reshape(total_rows, width)
     d_gate, d_up, g_gate, g_up, g_down = row_pass(x_rows, s_rows, gate_cols, up_cols, down_rows)

time: 460 us -> 493 us (1.072); the launches traced: 459 us -> 486 us
  blocking collectives: 109 us -> 194 us
  waiting for transfers between devices: 241 us -> 163 us
  local copies, waits for them, and re-layouts: 26.8 us -> 51.4 us
  matrix products: 42 us -> 36 us
    all_to_all x0 -> x1, blocking collectives: none -> 85.7 us  [hold_the_tokens(): front = lax.all_to_all(finding, axis_name='tp', split_axis=0, concat_axis=0)]
    all_gather x1 -> x0, waiting for transfers between devices: 70.3 us -> none  [per_device(): lax.all_gather(s_recv, 'tp', axis=2, tiled=True)]
    reshape x0 -> x1, local copies, waits for them, and re-layouts: none -> 15.5 us  [hold_the_tokens(): parts_out = jnp.concatenate(front, axis=pos_dim)]
    unnamed x28 -> x37, local copies, waits for them, and re-layouts: 1.58 us -> 10.2 us
    all_gather x1, waiting for transfers between devices: 7.21 us -> 0.01 us  [per_device(): lax.all_gather(x_recv, 'tp', axis=2, tiled=True)]
  transfers between devices with their start and end apart: 4 -> 3, of which waited for: 4 -> 2; matrix products, arithmetic and copies ran while one was open for 9% -> 11% of each run, Pallas kernels for 0% -> 0%
where the time goes in v1:
time: 493 us; the launch traced here: 486 us
  blocking collectives  194 us (39%)
  waiting for transfers between devices  163 us (33%)
  local copies, waits for them, and re-layouts  51.4 us (10%)
  matrix products  36 us (7%)
  other arithmetic  15.5 us (3%)
  between operations  14.6 us (3%)
  starting transfers between devices  11.3 us (2%)
    reduce_scatter x1, waiting for transfers between devices, per_device(): dx_rows = lax.psum_scatter(part, 'tp', scatter_dimension=1, tiled=True)  135 us
    all_to_all x1, blocking collectives, hold_the_tokens(): front = lax.all_to_all(finding, axis_name='tp', split_axis=0, concat_axis=0)  85.7 us
    all_to_all x1, blocking collectives, per_device(): lax.all_to_all(x_send, 'ep', split_axis=0, concat_axis=0, tiled=True)  57.5 us
    all_to_all x1, blocking collectives, per_device(): lax.all_to_all(s_send, 'ep', split_axis=0, concat_axis=0, tiled=True)  50.9 us
    all_to_all x1, waiting for transfers between devices, per_device(): lax.all_to_all(dx_rows.reshape(n_src, cap, quarter), 'ep', split_axis=0,...  28.3 us
    dot_general x3, matrix products, contract_first(): lax.dot_general(left, right, (((0,), (0,)), ((), ())), preferred_element_...  16.5 us
    reshape x1, local copies, waits for them, and re-layouts, hold_the_tokens(): parts_out = jnp.concatenate(front, axis=pos_dim)  15.5 us
    dot_general x3, matrix products, contract_last(): lax.dot_general(left, right, (((1,), (1,)), ((), ())), preferred_element_...  12 us
  transfers between devices with their start and end apart: 3, of which 2 were waited for; matrix products, arithmetic and copies ran while one was open for 11% of the time, Pallas kernels for 0%

profile of v1, /device:TPU:2, one launch (start us, length us, event | category | flops | bytes accessed | tf_op | source)
XLA Modules:
  0.0 486.0 jit_solution(2356060741169689674)
XLA Ops:
  11.1 2.4 scatter_custom_fusion
  13.7 5.3 %gather_fusion.1 = bf16[1024,896]{1,0:T(8,128)(2,1)} fusion(bf16[256,896]{1,0:T(8,128)(2,1)S(1)} %copy-done.2, s32[1024]{0:T(1024)S(1)} %get-tuple-element.9), kind=kCustom, calls=%fused_computation.1 | custom fusion | bytes 3674112 | tf_op jit(solution)/shard_map/jit(_take)/gather | solution.py:67
  20.8 57.5 %all_to_all.20 = bf16[64,16,896]{2,1,0:T(8,128)(2,1)} all-to-all(bf16[64,16,896]{2,1,0:T(8,128)(2,1)S(1)} %broadcast_select_fusion), channel_id=1, replica_groups=mesh['ep'=64,'tp'=4] {'ep'}, dimensions={0} | all-to-all | bytes 3670016 | tf_op jit(solution)/shard_map/all_to_all | solution.py:77
  81.1 3.4 mul.68
  86.1 5.3 %gather_fusion = bf16[1024,896]{1,0:T(8,128)(2,1)} fusion(bf16[512,896]{1,0:T(8,128)(2,1)S(1)} %multiply_convert_fusion, s32[1024]{0:T(1024)S(1)} %get-tuple-element.8), kind=kCustom, calls=%fused_computation | custom fusion | bytes 3674112 | tf_op jit(solution)/shard_map/jit(_take)/gather | solution.py:73
  91.4 1.9 broadcast_select_fusion.1
  93.3 50.9 %all_to_all.21 = bf16[64,16,896]{2,1,0:T(8,128)(2,1)S(1)} all-to-all(bf16[64,16,896]{2,1,0:T(8,128)(2,1)S(1)} %broadcast_select_fusion.1), channel_id=1, replica_groups=mesh['ep'=64,'tp'=4] {'ep'}, dimensions={0} | all-to-all | bytes 3670016 | tf_op jit(solution)/shard_map/all_to_all | solution.py:78
  144.8 85.7 %all_to_all.22 = bf16[4,64,16,896]{3,2,1,0:T(8,128)(2,1)} all-to-all(bf16[4,64,16,896]{3,2,1,0:T(8,128)(2,1)S(1)} %stack.2), channel_id=1, replica_groups=mesh['ep'=64,'tp'=4] {'tp'}, dimensions={0} | all-to-all | bytes 14680064 | tf_op jit(solution)/shard_map/all_to_all | solution.py:42
  230.5 15.5 %copy.30 = bf16[64,16,4,896]{3,2,1,0:T(4,128)(2,1)} copy(bf16[64,16,4,896]{3,1,0,2:T(8,128)(2,1)} %bitcast.62) | data formatting | bytes 14680064 | tf_op jit(solution)/shard_map/reshape | solution.py:43
  245.9 7.3 %copy.32 = bf16[128,8,4,896]{3,1,2,0:T(8,128)(2,1)} copy(bf16[128,8,4,896]{3,2,1,0:T(4,128)(2,1)} %bitcast.63) | data formatting | bytes 14680064
  253.3 5.5 %fusion.5 = f32[1024,256]{1,0:T(8,128)S(1)} fusion(bf16[1024,3584]{1,0:T(8,128)(2,1)} %bitcast.75, bf16[1,3584,256]{2,1,0:T(8,128)(2,1)S(1)} %copy-done), kind=kOutput, calls=%fused_computation.13 | convolution fusion | flops 1879048192 | bytes 10223616 | tf_op jit(solution)/shard_map/dot_general | solution.py:20
  259.0 2.1 fusion.8
  262.1 2.3 multiply_convert_fusion.2
  264.4 2.1 fusion.3
  266.5 7.6 %convolution_add_fusion = f32[1024,3584]{1,0:T(8,128)} fusion(f32[1024,3584]{1,0:T(8,128)S(1)} %fusion.3, bf16[1024,256]{1,0:T(8,128)(2,1)S(1)} %get-tuple-element.4, bf16[1,3584,256]{2,1,0:T(8,128)(2,1)S(1)} %copy-done.3), kind=kOutput, calls=%fused_computation.4 | convolution fusion | flops 1882718208 | bytes 31719424 | tf_op jit(solution)/shard_map/dot_general | solution.py:8
  274.1 134.8 %reduce-scatter.2.cloned.1.call-done = f32[1024,896]{1,0:T(8,128)} async-done(((f32[1024,3584]{1,0:T(8,128)}), f32[1024,896]{1,0:T(8,128)}) %reduce-scatter.2.cloned.1.call-update) | async-done | bytes 3670032 | tf_op jit(solution)/shard_map/reduce_scatter | solution.py:85
  408.9 3.5 convert_element_type.44
  412.4 11.2 %all-to-all-start.3 = ((bf16[64,16,896]{2,1,0:T(8,128)(2,1)}), bf16[64,16,896]{2,1,0:T(8,128)(2,1)}, u32[]{:S(2)}, u32[]{:S(2)}) async-start(bf16[64,16,896]{2,1,0:T(8,128)(2,1)} %bitcast.10), calls=%async_computation.4 | async-start | bytes 3670016 | tf_op jit(solution)/shard_map/all_to_all | solution.py:87
  424.0 6.6 %fusion.1 = bf16[1,3584,256]{2,1,0:T(8,128)(2,1)} fusion(bf16[1024,3584]{1,0:T(8,128)(2,1)} %bitcast.76, bf16[1024,256]{1,0:T(8,128)(2,1)S(1)} %get-tuple-element.4), kind=kOutput, calls=%fused_computation.9 | convolution fusion | flops 1879965696 | bytes 9699328 | tf_op jit(solution)/shard_map/dot_general | solution.py:14
  430.6 6.6 %fusion = bf16[1,3584,256]{2,1,0:T(8,128)(2,1)} fusion(bf16[1024,3584]{1,0:T(8,128)(2,1)} %bitcast.77, bf16[1024,256]{1,0:T(8,128)(2,1)S(1)} %get-tuple-element.5), kind=kOutput, calls=%fused_computation.8 | convolution fusion | flops 1879965696 | bytes 9699328 | tf_op jit(solution)/shard_map/dot_general | solution.py:14
  437.3 3.4 fusion.2
  440.6 28.3 %all-to-all-done.3 = bf16[64,16,896]{2,1,0:T(8,128)(2,1)} async-done(((bf16[64,16,896]{2,1,0:T(8,128)(2,1)}), bf16[64,16,896]{2,1,0:T(8,128)(2,1)}, u32[]{:S(2)}, u32[]{:S(2)}) %all-to-all-start.3) | async-done | bytes 1835040 | tf_op jit(solution)/shard_map/all_to_all | solution.py:87
  469.0 4.4 gather_fusion.2
  474.6 4.3 fusion.13
  (71 shorter events, 13.7 us)
Async XLA Ops:
  7.2 246.1 %copy-start = (bf16[1,3584,256]{2,1,0:T(8,128)(2,1)S(1)}, bf16[1,3584,256]{2,1,0:T(8,128)(2,1)}, u32[]{:S(2)}) copy-start(bf16[1,3584,256]{2,1,0:T(8,128)(2,1)} %param.11) | copy-start | bytes 5505028
  7.2 6.5 %copy-start.2 = (bf16[256,896]{1,0:T(8,128)(2,1)S(1)}, bf16[256,896]{1,0:T(8,128)(2,1)}, u32[]{:S(2)}) copy-start(bf16[256,896]{1,0:T(8,128)(2,1)} %param.7) | copy-start | bytes 1376260
  7.2 246.1 %all-gather.2.cloned.1.call-start = ((), (), s32[]{:S(2)}) async-start(), calls=%async_computation.5 | async-start | bytes 9175040 | tf_op jit(solution)/shard_map/all_gather | solution.py:80
  78.3 0.7 copy-start.6
  78.3 1.0 copy-start.4
  78.4 330.5 %reduce-scatter.2.cloned.1.call-start = ((), (), s32[]{:S(2)}) async-start(), calls=%async_computation.6 | async-start | bytes 18350080 | tf_op jit(solution)/shard_map/reduce_scatter | solution.py:85
  253.2 5.5 %copy-start.3 = (bf16[1,3584,256]{2,1,0:T(8,128)(2,1)S(1)}, bf16[1,3584,256]{2,1,0:T(8,128)(2,1)}, u32[]{:S(2)}) copy-start(bf16[1,3584,256]{2,1,0:T(8,128)(2,1)} %param.12) | copy-start | bytes 5505028
  253.3 5.7 %copy-start.7 = (bf16[64,16,3584]{2,1,0:T(8,128)(2,1)S(1)}, bf16[64,16,3584]{2,1,0:T(8,128)(2,1)}, u32[]{:S(2)}) copy-start(bf16[64,16,3584]{2,1,0:T(8,128)(2,1)} %all-gather.2.cloned.1.call-done) | copy-start | bytes 22020100
  253.3 7.8 %slice-start = ((s8[7340032]{0:T(1024)(128)(4,1)}), s8[4194304]{0:T(1024)(128)(4,1)S(1)}, s32[]{:S(2)}) async-start(s8[7340032]{0:T(1024)(128)(4,1)} %bitcast.66), calls=%async_computation.7 | async-start | bytes 8388608
  259.0 2.1 copy-start.9
  259.0 2.6 slice-start.1
  259.0 3.1 copy-start.8
  261.1 3.3 copy-start.11
  412.4 11.5 %copy-start.5 = (s32[256,2]{0,1:T(2,128)S(1)}, s32[256,2]{0,1:T(2,128)}, u32[]{:S(2)}) copy-start(s32[256,2]{0,1:T(2,128)} %param.9) | copy-start | bytes 6148
  412.4 56.6 %all-to-all-start.3 = ((bf16[64,16,896]{2,1,0:T(8,128)(2,1)}), bf16[64,16,896]{2,1,0:T(8,128)(2,1)}, u32[]{:S(2)}, u32[]{:S(2)}) async-start(bf16[64,16,896]{2,1,0:T(8,128)(2,1)} %bitcast.10), calls=%async_computation.4 | async-start | bytes 3670016 | tf_op jit(solution)/shard_map/all_to_all | solution.py:87
  424.0 13.2 %slice-start.2 = ((s8[7340032]{0:T(1024)(128)(4,1)}), s8[4194304]{0:T(1024)(128)(4,1)S(1)}, s32[]{:S(2)}) async-start(s8[7340032]{0:T(1024)(128)(4,1)} %bitcast.69), calls=%async_computation.9 | async-start | bytes 8388608
  430.6 6.6 %slice-start.3 = ((s8[7340032]{0:T(1024)(128)(4,1)}), s8[3145728]{0:T(1024)(128)(4,1)S(1)}, s32[]{:S(2)}) async-start(s8[7340032]{0:T(1024)(128)(4,1)} %bitcast.69), calls=%async_computation.10 | async-start | bytes 6291456
  430.6 6.6 %copy-start.10 = (f32[1024,256]{1,0:T(8,128)S(1)}, f32[1024,256]{1,0:T(8,128)}, u32[]{:S(2)}) copy-start(f32[1024,256]{1,0:T(8,128)} %copy-done.9) | copy-start | bytes 3145732
  430.6 6.6 %copy-start.12 = (f32[1024,256]{1,0:T(8,128)S(1)}, f32[1024,256]{1,0:T(8,128)}, u32[]{:S(2)}) copy-start(f32[1024,256]{1,0:T(8,128)} %copy-done.11) | copy-start | bytes 3145732
  469.0 10.0 %copy-start.1 = (bf16[1,3584,256]{2,1,0:T(8,128)(2,1)S(1)}, bf16[1,3584,256]{2,1,0:T(8,128)(2,1)}, u32[]{:S(2)}) copy-start(bf16[1,3584,256]{2,1,0:T(8,128)(2,1)} %param.11) | copy-start | bytes 5505028
Sparse Core Ops, SparseCore 0:
  78.5 73.8 all-gather.1
  274.3 134.5 reduce-scatter.1
